TPU v7x, 256 devices: a whole 4x4x8 slice. The times are simulated.
256 devices in a mesh: ctx: 16 (over y_hi, x, core), dp: 16 (over y_lo, z).
Axes of the slice: x: 4, y: 4 (y_hi: 2, y_lo: 2; y = y_hi * 2 + y_lo), z: 8, core: 2. Of those that a mesh axis runs over, the one named last changes fastest.
Arguments:
- queries: bfloat16 [16, 2048, 1536], P('dp', 'ctx'), as said below
- keys: bfloat16 [16, 2048, 1536], P('dp', 'ctx'), as said below
- values: bfloat16 [16, 2048, 1536], P('dp', 'ctx'), may hold values from -6 to 6
- tangent_queries: bfloat16 [16, 2048, 1536], P('dp', 'ctx'), may hold values from -6 to 6
- tangent_keys: bfloat16 [16, 2048, 1536], P('dp', 'ctx'), may hold values from -6 to 6
- tangent_values: bfloat16 [16, 2048, 1536], P('dp', 'ctx'), may hold values from -6 to 6
- clip_ids: int32 [16, 2048], P('dp', 'ctx'), may hold values from 0 to 3, never falling along the last dimension, each value on 1 to 1024 neighbouring positions
- block_order: int32 [16], replicated, may hold values from 0 to 15, each once
- out_weight: bfloat16 [1536, 3072], replicated, may hold values from -0.15625 to 0.15625
- layer_scale: float32 [3072], replicated, may hold values from 0.1 to 1.9
- cotangent: bfloat16 [16, 2048, 3072], P('dp', 'ctx'), as said below
Outputs:
- tangent_branch: bfloat16 [16, 2048, 3072], P('dp', 'ctx')
- scale_grad: float32 [3072], replicated
Inputs may be any that keep to these rules, and one draw needn't show every extreme that they name: `clip_ids`: ids never fall along a sample's rows; each of the 4 clips is a run of consecutive rows. `block_order`: each block number appears once. `queries`: real-valued. `keys`: real-valued. `cotangent`: real-valued.
All inputs are finite; a program needn't handle non-finite values.
Results may differ from a plain program's by a relative error of at most 0.02.
The roundings to bfloat16 on the way count: a program that leaves them out, or rounds other values in their place, can miss the bound.
Values may be sent and summed in bfloat16 or wider, within the bound.
A program may use at most 192 MiB of HBM per device.

v0:
```python
import math

import jax
import jax.numpy as jnp
from jax import lax
from jax.sharding import PartitionSpec as P

HEADS = 12


def rotate(x, pos, half_dim):
    frequency = 10000.0 ** (-jnp.arange(half_dim, dtype=jnp.float32) / half_dim)
    angles = pos.astype(jnp.float32)[:, None] * frequency[None, :]
    cosine = jnp.cos(angles)[:, None, :]
    sine_part = jnp.sin(angles)[:, None, :]
    front_part = x[..., :half_dim]
    back_part = x[..., half_dim:]
    return jnp.concatenate(
        [front_part * cosine - back_part * sine_part, back_part * cosine + front_part * sine_part],
        axis=-1,
    )


def make_attend(query_rot, tquery_rot, query_ids, scale):

    def attend(carry, block):
        best, total, weighted, primal_acc, slope_acc, spread_acc = carry
        key_blk, value_blk, tkey_blk, tvalue_blk, key_ids = block
        scores = (
            jnp.einsum("hqd,hkd->hqk", query_rot, key_blk, preferred_element_type=jnp.float32)
            * scale
        )
        same_clip = query_ids[:, None] == key_ids[None, :]
        scores = jnp.where(same_clip[None], scores, -jnp.inf)
        slopes = (
            jnp.einsum("hqd,hkd->hqk", tquery_rot, key_blk, preferred_element_type=jnp.float32)
            + jnp.einsum("hqd,hkd->hqk", query_rot, tkey_blk, preferred_element_type=jnp.float32)
        ) * scale
        new_best = jnp.maximum(best, jnp.max(scores, axis=-1))
        factor = jnp.exp(best - new_best)
        weights = jnp.exp(scores - new_best[..., None])
        tilted = weights * slopes
        total = total * factor + jnp.sum(weights, axis=-1)
        weighted = weighted * factor + jnp.sum(tilted, axis=-1)
        weights_b = weights.astype(jnp.bfloat16)
        tilted_b = tilted.astype(jnp.bfloat16)
        primal_acc = primal_acc * factor[..., None] + jnp.einsum(
            "hqk,hkd->hqd", weights_b, value_blk, preferred_element_type=jnp.float32
        )
        slope_acc = slope_acc * factor[..., None] + jnp.einsum(
            "hqk,hkd->hqd", tilted_b, value_blk, preferred_element_type=jnp.float32
        )
        spread_acc = spread_acc * factor[..., None] + jnp.einsum(
            "hqk,hkd->hqd", weights_b, tvalue_blk, preferred_element_type=jnp.float32
        )
        return ((new_best, total, weighted, primal_acc, slope_acc, spread_acc), None)

    return attend


def start_states(heads, rows, head_dim):
    zeros_rows = jnp.zeros((heads, rows), jnp.float32)
    zeros_heads = jnp.zeros((heads, rows, head_dim), jnp.float32)
    return (
        jnp.full((heads, rows), -1e30, jnp.float32),
        zeros_rows,
        zeros_rows,
        zeros_heads,
        zeros_heads,
        zeros_heads,
    )


def local(
    queries,
    keys,
    values,
    tangent_queries,
    tangent_keys,
    tangent_values,
    clip_ids,
    block_order,
    out_weight,
    layer_scale,
    cotangent,
):
    tok_rows = queries.shape[1]
    heads = HEADS
    head_dim = queries.shape[2] // heads
    scale = head_dim ** (-0.5)
    cycle_index = lax.axis_index("ctx")
    positions = block_order[cycle_index] * tok_rows + jnp.arange(tok_rows, dtype=jnp.int32)

    def heads_first(x, turned):
        y = x[0].reshape(tok_rows, heads, head_dim)
        if turned:
            y = rotate(y.astype(jnp.float32), positions, head_dim // 2).astype(jnp.bfloat16)
        return jnp.transpose(y, (1, 0, 2))

    query_rot = heads_first(queries, True)
    key_rot = heads_first(keys, True)
    value_heads = heads_first(values, False)
    tquery_rot = heads_first(tangent_queries, True)
    tkey_rot = heads_first(tangent_keys, True)
    tvalue_heads = heads_first(tangent_values, False)
    all_ids = lax.all_gather(clip_ids, "ctx", axis=1, tiled=True)[0]
    own_ids = clip_ids[0]
    attend = make_attend(query_rot, tquery_rot, own_ids, scale)
    carry = start_states(heads, tok_rows, head_dim)
    key_part = lax.all_gather(key_rot, "ctx", axis=1, tiled=True)
    value_part = lax.all_gather(value_heads, "ctx", axis=1, tiled=True)
    tkey_part = lax.all_gather(tkey_rot, "ctx", axis=1, tiled=True)
    tvalue_part = lax.all_gather(tvalue_heads, "ctx", axis=1, tiled=True)
    count = key_part.shape[1]
    block_rows = math.gcd(count, tok_rows)
    blocks = count // block_rows

    def split_blocks(x):
        return jnp.transpose(x.reshape(heads, blocks, block_rows, head_dim), (1, 0, 2, 3))

    stacked = (
        split_blocks(key_part),
        split_blocks(value_part),
        split_blocks(tkey_part),
        split_blocks(tvalue_part),
        all_ids.reshape(blocks, block_rows),
    )
    carry, unused = lax.scan(attend, carry, stacked)
    best, total, weighted, primal_acc, slope_acc, spread_acc = carry
    mean_out = primal_acc / total[..., None]
    tangent_heads = (
        (slope_acc + spread_acc) / total[..., None] - (weighted / total)[..., None] * mean_out
    ).astype(jnp.bfloat16)
    tangent_rows = jnp.transpose(tangent_heads, (1, 0, 2)).reshape(tok_rows, heads * head_dim)
    projected = jnp.dot(tangent_rows, out_weight, preferred_element_type=jnp.float32)
    branch = (layer_scale * projected).astype(jnp.bfloat16)[None]
    partial_grad = jnp.sum(cotangent[0].astype(jnp.float32) * projected, axis=0)
    summed = lax.psum(partial_grad, ("ctx", "dp"))
    count_all = lax.axis_size("ctx") * lax.axis_size("dp") * tok_rows
    return (branch, summed / math.sqrt(count_all))


def solution(mesh):
    in_specs = (
        P("dp", "ctx", None),
        P("dp", "ctx", None),
        P("dp", "ctx", None),
        P("dp", "ctx", None),
        P("dp", "ctx", None),
        P("dp", "ctx", None),
        P("dp", "ctx"),
        P(),
        P(),
        P(),
        P("dp", "ctx", None),
    )
    out_specs = (P("dp", "ctx", None), P())
    return jax.shard_map(local, mesh=mesh, in_specs=in_specs, out_specs=out_specs, check_vma=False)
```

profile of v0, /device:TPU:1, one launch (start us, length us, event | category | flops | bytes accessed | tf_op | source)
XLA Modules:
  0.0 623.5 jit_solution(16415383374081786712)
XLA Ops:
  18.6 1.9 copy.28
  22.8 25.8 %all_gather.15 = s32[1,2048]{1,0:T(1,128)} all-gather(s32[1,128]{1,0:T(1,128)} %param.19), channel_id=1, replica_groups=mesh['ctx'=16,'dp'=16] {'ctx'}, dimensions={1}, use_global_device_ids=true | all-gather | bytes 8704 | tf_op jit(solution)/shard_map/all_gather | solution.py:106
  48.7 46.9 %all-gather.5.cloned.1.call-done = bf16[12,2048,128]{1,2,0:T(8,128)(2,1)} async-done(((bf16[12,128,128]{1,2,0:T(8,128)(2,1)}), bf16[12,2048,128]{1,2,0:T(8,128)(2,1)}) %all-gather.5.cloned.1.call-update) | async-done | bytes 6291472 | tf_op jit(solution)/shard_map/all_gather | solution.py:110
  95.6 7.8 %copy.44 = bf16[192,8,16,128]{3,2,1,0:T(8,128)(2,1)} copy(bf16[192,8,16,128]{3,1,2,0:T(8,128)(2,1)} %bitcast.120) | data formatting | bytes 12582912
  103.3 9.0 %copy.21 = bf16[12,16,128,128]{3,2,0,1:T(8,128)(2,1)} copy(bf16[12,16,128,128]{2,1,3,0:T(8,128)(2,1)} %bitcast.115) | data formatting | bytes 12582912 | tf_op jit(solution)/shard_map/reshape | solution.py:119
  112.4 58.9 %all-gather.7.cloned.1.call-done = bf16[12,2048,128]{1,2,0:T(8,128)(2,1)} async-done(((bf16[12,128,128]{1,2,0:T(8,128)(2,1)}), bf16[12,2048,128]{1,2,0:T(8,128)(2,1)}) %all-gather.7.cloned.1.call-update) | async-done | bytes 6291472 | tf_op jit(solution)/shard_map/all_gather | solution.py:112
  171.3 8.7 %copy.25 = bf16[12,2048,128]{2,1,0:T(8,128)(2,1)} copy(bf16[12,2048,128]{1,2,0:T(8,128)(2,1)} %all-gather.7.cloned.1.call-done) | data formatting | bytes 12582912 | tf_op jit(solution)/shard_map/all_gather | solution.py:112
  180.0 67.1 %all-gather.9.cloned.1.call-done = bf16[12,2048,128]{1,2,0:T(8,128)(2,1)} async-done(((bf16[12,128,128]{1,2,0:T(8,128)(2,1)}), bf16[12,2048,128]{1,2,0:T(8,128)(2,1)}) %all-gather.9.cloned.1.call-update) | async-done | bytes 6291472 | tf_op jit(solution)/shard_map/all_gather | solution.py:111
  247.1 8.6 %copy.27 = bf16[12,2048,128]{2,1,0:T(8,128)(2,1)} copy(bf16[12,2048,128]{1,2,0:T(8,128)(2,1)} %all-gather.9.cloned.1.call-done) | data formatting | bytes 12582912 | tf_op jit(solution)/shard_map/all_gather | solution.py:111
  255.7 67.0 %all-gather.11.cloned.1.call-done = bf16[12,2048,128]{1,2,0:T(8,128)(2,1)} async-done(((bf16[12,128,128]{1,2,0:T(8,128)(2,1)}), bf16[12,2048,128]{1,2,0:T(8,128)(2,1)}) %all-gather.11.cloned.1.call-update) | async-done | bytes 6291472 | tf_op jit(solution)/shard_map/all_gather | solution.py:113
  322.7 8.7 %copy.29 = bf16[12,2048,128]{2,1,0:T(8,128)(2,1)} copy(bf16[12,2048,128]{1,2,0:T(8,128)(2,1)} %all-gather.11.cloned.1.call-done) | data formatting | bytes 12582912 | tf_op jit(solution)/shard_map/all_gather | solution.py:113
  331.3 200.5 %while.21 = (s32[]{:T(128)}, f32[12,128]{1,0:T(8,128)S(1)}, f32[12,128]{1,0:T(8,128)}, f32[12,128]{1,0:T(8,128)}, f32[12,128,128]{2,1,0:T(8,128)S(1)}, /*index=5...) while((s32[]{:T(128)}, f32[12,128]{1,0:T(8,128)S(1)}, ...), condition=%wide.region_4.5_spmd.clone, body=%wide.region_0.4_spmd.clone.sunk | while | flops 306735616 | bytes 14789864 | solution.py:128
  337.8 1.6 convolution_add_fusion.9
  339.3 1.6 convolution_add_fusion.8
  340.9 1.6 convolution_add_fusion.7
  350.3 1.6 convolution_add_fusion.9
  351.9 1.6 convolution_add_fusion.8
  353.5 1.6 convolution_add_fusion.7
  362.9 1.6 convolution_add_fusion.9
  364.5 1.6 convolution_add_fusion.8
  366.0 1.6 convolution_add_fusion.7
  375.5 1.6 convolution_add_fusion.9
  377.0 1.6 convolution_add_fusion.8
  378.6 1.6 convolution_add_fusion.7
  388.1 1.6 convolution_add_fusion.9
  389.6 1.6 convolution_add_fusion.8
  391.2 1.6 convolution_add_fusion.7
  400.6 1.6 convolution_add_fusion.9
  402.2 1.6 convolution_add_fusion.8
  403.8 1.6 convolution_add_fusion.7
  413.2 1.6 convolution_add_fusion.9
  414.8 1.6 convolution_add_fusion.8
  416.3 1.6 convolution_add_fusion.7
  425.8 1.6 convolution_add_fusion.9
  427.4 1.6 convolution_add_fusion.8
  428.9 1.6 convolution_add_fusion.7
  438.4 1.6 convolution_add_fusion.9
  439.9 1.6 convolution_add_fusion.8
  441.5 1.6 convolution_add_fusion.7
  446.7 1.5 fusion.72
  450.9 1.6 convolution_add_fusion.9
  452.5 1.6 convolution_add_fusion.8
  454.1 1.6 convolution_add_fusion.7
  463.5 1.6 convolution_add_fusion.9
  465.1 1.6 convolution_add_fusion.8
  466.6 1.6 convolution_add_fusion.7
  476.1 1.6 convolution_add_fusion.9
  477.6 1.6 convolution_add_fusion.8
  479.2 1.6 convolution_add_fusion.7
  488.6 1.6 convolution_add_fusion.9
  490.2 1.6 convolution_add_fusion.8
  491.8 1.6 convolution_add_fusion.7
  501.2 1.6 convolution_add_fusion.9
  502.8 1.6 convolution_add_fusion.8
  504.3 1.6 convolution_add_fusion.7
  513.8 1.6 convolution_add_fusion.9
  515.3 1.6 convolution_add_fusion.8
  516.9 1.6 convolution_add_fusion.7
  522.1 1.5 fusion.72
  526.4 1.6 convolution_add_fusion.9
  527.9 1.6 convolution_add_fusion.8
  529.5 1.6 convolution_add_fusion.7
  534.3 6.4 %fusion.32 = (f32[3072]{0:T(1024)S(1)}, bf16[1,128,3072]{2,1,0:T(8,128)(2,1)}) fusion(bf16[1,128,3072]{2,1,0:T(8,128)(2,1)} %param.23, f32[3072]{0:T(1024)S(1)} %copy-done.3, bf16[128,1536]{0,1:T(8,128)(2,1)S(1)} %bitcast.121, bf16[1536,3072]{1,0:T(8,128)(2,1)} %param.21), kind=kOutput, calls=%fused_computation.46 | convolution fusion | flops 1209922560 | bytes 11427840 | tf_op jit(solution)/shard_map/dot_general | solution.py:135
  540.7 75.7 %psum.7 = f32[3072]{0:T(1024)S(1)} all-reduce(f32[3072]{0:T(1024)S(1)} %get-tuple-element.187), channel_id=1, replica_groups=mesh['ctx'=16,'dp'=16] {'ctx','dp'}, use_global_device_ids=true, to_apply=%region_6.7 | all-reduce | flops 3072 | bytes 24576 | tf_op jit(solution)/shard_map/psum | solution.py:138
  (265 shorter events, 136.7 us)
Async XLA Ops:
  7.2 88.4 %all-gather.5.cloned.1.call-start = ((), (), s32[]{:S(2)}) async-start(), calls=%async_computation | async-start | bytes 6684672 | tf_op jit(solution)/shard_map/all_gather | solution.py:110
  11.7 5.9 copy-start.2
  16.6 154.7 %all-gather.7.cloned.1.call-start = ((), (), s32[]{:S(2)}) async-start(), calls=%async_computation.1 | async-start | bytes 6684672 | tf_op jit(solution)/shard_map/all_gather | solution.py:112
  17.5 229.6 %all-gather.9.cloned.1.call-start = ((), (), s32[]{:S(2)}) async-start(), calls=%async_computation.2 | async-start | bytes 6684672 | tf_op jit(solution)/shard_map/all_gather | solution.py:111
  18.5 304.1 %all-gather.11.cloned.1.call-start = ((), (), s32[]{:S(2)}) async-start(), calls=%async_computation.3 | async-start | bytes 6684672 | tf_op jit(solution)/shard_map/all_gather | solution.py:113
  334.2 8.4 %copy-start = (f32[12,128]{1,0:T(8,128)S(1)}, f32[12,128]{1,0:T(8,128)}, u32[]{:S(2)}) copy-start(f32[12,128]{1,0:T(8,128)} %get-tuple-element.331) | copy-start | bytes 18436 | tf_op jit(solution)/shard_map/while
  342.6 0.6 copy-start.1
  346.1 9.1 %copy-start = (f32[12,128]{1,0:T(8,128)S(1)}, f32[12,128]{1,0:T(8,128)}, u32[]{:S(2)}) copy-start(f32[12,128]{1,0:T(8,128)} %get-tuple-element.331) | copy-start | bytes 18436 | tf_op jit(solution)/shard_map/while
  355.2 0.6 copy-start.1
  358.6 9.1 %copy-start = (f32[12,128]{1,0:T(8,128)S(1)}, f32[12,128]{1,0:T(8,128)}, u32[]{:S(2)}) copy-start(f32[12,128]{1,0:T(8,128)} %get-tuple-element.331) | copy-start | bytes 18436 | tf_op jit(solution)/shard_map/while
  367.8 0.6 copy-start.1
  371.2 9.1 %copy-start = (f32[12,128]{1,0:T(8,128)S(1)}, f32[12,128]{1,0:T(8,128)}, u32[]{:S(2)}) copy-start(f32[12,128]{1,0:T(8,128)} %get-tuple-element.331) | copy-start | bytes 18436 | tf_op jit(solution)/shard_map/while
  380.3 0.6 copy-start.1
  383.8 9.1 %copy-start = (f32[12,128]{1,0:T(8,128)S(1)}, f32[12,128]{1,0:T(8,128)}, u32[]{:S(2)}) copy-start(f32[12,128]{1,0:T(8,128)} %get-tuple-element.331) | copy-start | bytes 18436 | tf_op jit(solution)/shard_map/while
  392.9 0.6 copy-start.1
  396.4 9.1 %copy-start = (f32[12,128]{1,0:T(8,128)S(1)}, f32[12,128]{1,0:T(8,128)}, u32[]{:S(2)}) copy-start(f32[12,128]{1,0:T(8,128)} %get-tuple-element.331) | copy-start | bytes 18436 | tf_op jit(solution)/shard_map/while
  405.5 0.6 copy-start.1
  408.9 9.1 %copy-start = (f32[12,128]{1,0:T(8,128)S(1)}, f32[12,128]{1,0:T(8,128)}, u32[]{:S(2)}) copy-start(f32[12,128]{1,0:T(8,128)} %get-tuple-element.331) | copy-start | bytes 18436 | tf_op jit(solution)/shard_map/while
  418.1 0.6 copy-start.1
  421.5 9.1 %copy-start = (f32[12,128]{1,0:T(8,128)S(1)}, f32[12,128]{1,0:T(8,128)}, u32[]{:S(2)}) copy-start(f32[12,128]{1,0:T(8,128)} %get-tuple-element.331) | copy-start | bytes 18436 | tf_op jit(solution)/shard_map/while
  430.6 0.6 copy-start.1
  434.1 9.1 %copy-start = (f32[12,128]{1,0:T(8,128)S(1)}, f32[12,128]{1,0:T(8,128)}, u32[]{:S(2)}) copy-start(f32[12,128]{1,0:T(8,128)} %get-tuple-element.331) | copy-start | bytes 18436 | tf_op jit(solution)/shard_map/while
  443.2 0.6 copy-start.1
  446.7 9.1 %copy-start = (f32[12,128]{1,0:T(8,128)S(1)}, f32[12,128]{1,0:T(8,128)}, u32[]{:S(2)}) copy-start(f32[12,128]{1,0:T(8,128)} %get-tuple-element.331) | copy-start | bytes 18436 | tf_op jit(solution)/shard_map/while
  455.8 0.6 copy-start.1
  459.2 9.1 %copy-start = (f32[12,128]{1,0:T(8,128)S(1)}, f32[12,128]{1,0:T(8,128)}, u32[]{:S(2)}) copy-start(f32[12,128]{1,0:T(8,128)} %get-tuple-element.331) | copy-start | bytes 18436 | tf_op jit(solution)/shard_map/while
  468.4 0.6 copy-start.1
  471.8 9.1 %copy-start = (f32[12,128]{1,0:T(8,128)S(1)}, f32[12,128]{1,0:T(8,128)}, u32[]{:S(2)}) copy-start(f32[12,128]{1,0:T(8,128)} %get-tuple-element.331) | copy-start | bytes 18436 | tf_op jit(solution)/shard_map/while
  480.9 0.6 copy-start.1
  484.4 9.1 %copy-start = (f32[12,128]{1,0:T(8,128)S(1)}, f32[12,128]{1,0:T(8,128)}, u32[]{:S(2)}) copy-start(f32[12,128]{1,0:T(8,128)} %get-tuple-element.331) | copy-start | bytes 18436 | tf_op jit(solution)/shard_map/while
  493.5 0.6 copy-start.1
  496.9 9.1 %copy-start = (f32[12,128]{1,0:T(8,128)S(1)}, f32[12,128]{1,0:T(8,128)}, u32[]{:S(2)}) copy-start(f32[12,128]{1,0:T(8,128)} %get-tuple-element.331) | copy-start | bytes 18436 | tf_op jit(solution)/shard_map/while
  506.1 0.6 copy-start.1
  509.5 9.1 %copy-start = (f32[12,128]{1,0:T(8,128)S(1)}, f32[12,128]{1,0:T(8,128)}, u32[]{:S(2)}) copy-start(f32[12,128]{1,0:T(8,128)} %get-tuple-element.331) | copy-start | bytes 18436 | tf_op jit(solution)/shard_map/while
  518.6 0.6 copy-start.1
  522.1 9.1 %copy-start = (f32[12,128]{1,0:T(8,128)S(1)}, f32[12,128]{1,0:T(8,128)}, u32[]{:S(2)}) copy-start(f32[12,128]{1,0:T(8,128)} %get-tuple-element.331) | copy-start | bytes 18436 | tf_op jit(solution)/shard_map/while
  531.2 0.6 copy-start.1
  531.8 2.5 copy-start.3
Sparse Core Ops, SparseCore 0:
  16.7 78.7 all-gather.4
  98.1 73.1 all-gather.6
  173.9 73.1 all-gather.8
  249.5 73.1 all-gather.10
where the time goes:
time: 630 us; the launch traced here: 623 us
  waiting for transfers between devices  240 us (38%)
  matrix products  150 us (24%)
  blocking collectives  102 us (16%)
  local copies, waits for them, and re-layouts  74 us (12%)
  other arithmetic  41 us (7%)
  between operations  14.6 us (2%)
    psum x1, blocking collectives, local(): summed = lax.psum(partial_grad, ('ctx', 'dp'))  75.7 us
    all_gather x1, waiting for transfers between devices, local(): value_part = lax.all_gather(value_heads, 'ctx', axis=1, tiled=True)  67.1 us
    all_gather x1, waiting for transfers between devices, local(): tvalue_part = lax.all_gather(tvalue_heads, 'ctx', axis=1, tiled=True)  67 us
    all_gather x1, waiting for transfers between devices, local(): tkey_part = lax.all_gather(tkey_rot, 'ctx', axis=1, tiled=True)  58.9 us
    all_gather x1, waiting for transfers between devices, local(): key_part = lax.all_gather(key_rot, 'ctx', axis=1, tiled=True)  46.9 us
    all_gather x1, blocking collectives, local(): all_ids = lax.all_gather(clip_ids, 'ctx', axis=1, tiled=True)[0]  25.8 us
    dot_general x16, matrix products, attend(): jnp.einsum('hqk,hkd->hqd', weights_b, value_blk, preferred_element_type=j...  25.1 us
    dot_general x16, matrix products, attend(): jnp.einsum('hqk,hkd->hqd', tilted_b, value_blk, preferred_element_type=jn...  24.9 us
  transfers between devices with their start and end apart: 4, of which 4 were waited for; matrix products, arithmetic and copies ran while one was open for 6% of the time, Pallas kernels for 0%

commit v1 on v0

v1 whole, which is shorter than its diff:
```python
import math

import jax
import jax.numpy as jnp
import numpy as np
from jax import lax
from jax.experimental import pallas as pl
from jax.experimental.pallas import tpu as pltpu
from jax.sharding import PartitionSpec as P

MESH = pl.DeviceIdType.MESH
HEADS = 12
HD = 128
ROWS = 128
F32 = jnp.float32
BF16 = jnp.bfloat16


def owner_of(head):
    row, rest = head // 6, head % 6
    return 8 * row + rest + (rest + 2 * row) // 3


def kernel(
    n_ctx,
    n_dp,
    order_ref,
    q_ref,
    k_ref,
    v_ref,
    tq_ref,
    tk_ref,
    tv_ref,
    ids_ref,
    turn_ref,
    block_turn_ref,
    w_ref,
    ls_ref,
    cot_ref,
    branch_ref,
    grad_ref,
    kk_stage,
    qq_stage,
    id_stage,
    kk,
    vv,
    qq,
    id_rows,
    id_cols,
    s_buf,
    wb_buf,
    tb_buf,
    out_stage,
    attn,
    w_buf,
    g_part,
    g_ctx,
    g_sum,
    g_dp,
    w_sem,
    send_k,
    send_v,
    send_tv,
    send_q,
    send_id,
    recv_k,
    recv_v,
    recv_q,
    recv_id,
    send_out,
    recv_out,
    send_gc,
    recv_gc,
    send_gd,
    recv_gd,
):
    me = lax.axis_index("ctx")
    me_dp = lax.axis_index("dp")
    chip, core = me // 2, me % 2
    row, col = chip // 4, chip % 4
    my_head = 6 * row + (3 * col + 1 - row) // 2 + core
    is_owner = core * ((row + col) % 2) == 0
    chips = n_ctx // 2

    w_copy = pltpu.make_async_copy(w_ref, w_buf, w_sem)
    w_copy.start()

    barrier = pltpu.get_barrier_semaphore()

    @pl.loop(1, n_ctx)
    def _(i):
        pl.semaphore_signal(
            barrier, inc=1, device_id={"ctx": (me + i) % n_ctx}, device_id_type=MESH
        )

    @pl.loop(1, n_dp)
    def _(i):
        pl.semaphore_signal(
            barrier, inc=1, device_id={"dp": (me_dp + i) % n_dp}, device_id_type=MESH
        )

    place = order_ref[me]
    cos_b = block_turn_ref[0, pl.ds(place, 1), :]
    sin_b = block_turn_ref[1, pl.ds(place, 1), :]
    cos_t, sin_t = turn_ref[0], turn_ref[1]
    lane = lax.broadcasted_iota(jnp.int32, (ROWS, HD), 1)
    cosine = cos_b * cos_t - sin_b * sin_t
    sine = sin_b * cos_t + cos_b * sin_t
    sine = jnp.where(lane < HD // 2, -sine, sine)

    def turned(x, c, s):
        x = x.astype(F32)
        return (x * c + pltpu.roll(x, HD // 2, axis=1) * s).astype(BF16)

    for h in range(HEADS):
        cols = slice(h * HD, (h + 1) * HD)
        kk_stage[h, :, 0:HD] = turned(k_ref[0, :, cols], cosine, sine)
        kk_stage[h, :, HD : 2 * HD] = turned(tk_ref[0, :, cols], cosine, sine)
    cosine, sine = cosine * 0.0625, sine * 0.0625
    for h in range(HEADS):
        cols = slice(h * HD, (h + 1) * HD)
        qq_stage[h, :, 0:HD] = turned(tq_ref[0, :, cols], cosine, sine)
        qq_stage[h, :, HD : 2 * HD] = turned(q_ref[0, :, cols], cosine, sine)
    id_stage[...] = jnp.broadcast_to(ids_ref[...].astype(F32), (8, HD))

    pl.semaphore_wait(barrier, n_ctx - 1 + n_dp - 1)

    rows_here = pl.ds(pl.multiple_of(me * ROWS, ROWS), ROWS)

    def pieces(h):
        cols = pl.ds(pl.multiple_of(h * HD, HD), HD)
        return [
            (id_stage, id_rows.at[me], send_id.at[h], recv_id),
            (kk_stage.at[h], kk.at[rows_here, :], send_k.at[h], recv_k),
            (v_ref.at[0, :, cols], vv.at[rows_here, pl.ds(0, HD)], send_v.at[h], recv_v),
            (tv_ref.at[0, :, cols], vv.at[rows_here, pl.ds(HD, HD)], send_tv.at[h], recv_v),
            (qq_stage.at[h], qq.at[rows_here, :], send_q.at[h], recv_q.at[me]),
        ]

    def remote(piece, to):
        src, dst, ssem, rsem = piece
        return pltpu.make_async_remote_copy(
            src_ref=src,
            dst_ref=dst,
            send_sem=ssem,
            recv_sem=rsem,
            device_id={"ctx": to},
            device_id_type=MESH,
        )

    def start_sends(which):
        @pl.loop(0, HEADS)
        def _(i):
            h = (i + my_head) % HEADS
            to = owner_of(h)

            @pl.when(to != me)
            def _():
                for p in which:
                    remote(pieces(h)[p], to).start()

            @pl.when(to == me)
            def _():
                for p in which:
                    src, dst, _, rsem = pieces(h)[p]
                    pltpu.make_async_copy(src, dst, rsem).start()

    start_sends((0, 1, 2, 3))
    start_sends((4,))

    @pl.when(is_owner)
    def _():
        pltpu.make_async_copy(id_rows, id_rows, recv_id).wait()

        @pl.loop(0, n_ctx)
        def _(j):
            ids = jnp.broadcast_to(id_rows[j, 0:1, :], (ROWS, HD))
            id_cols[pl.ds(pl.multiple_of(j * ROWS, ROWS), ROWS), :] = ids.T

        pltpu.make_async_copy(kk, kk, recv_k).wait()
        pltpu.make_async_copy(vv, vv, recv_v).wait()

        tile = 2 * ROWS
        step = math.log2(math.e) * math.sqrt(2.0)
        contract_last = (((1,), (1,)), ((), ()))

        @pl.loop(0, chips)
        def _(t):
            at = (chip + t) % chips
            rows = pl.ds(pl.multiple_of(at * tile, tile), tile)
            for c in range(2):
                block = at * 2 + c
                part = qq.at[pl.ds(pl.multiple_of(block * ROWS, ROWS), ROWS), :]
                pltpu.make_async_copy(part, part, recv_q.at[block]).wait()
            both = qq[rows, :]
            q = both[:, HD : 2 * HD]
            mine = id_cols[rows, :]
            best = jnp.full((tile, HD), -jnp.inf, F32)
            for c in range(chips):
                keys = kk[c * tile : (c + 1) * tile, 0:HD]
                s = lax.dot_general(q, keys, contract_last, preferred_element_type=F32)
                for half in range(2):
                    j = 2 * c + half
                    theirs = jnp.broadcast_to(id_rows[j, 0:1, :], (tile, HD))
                    s_half = jnp.where(mine == theirs, s[:, half * HD : (half + 1) * HD], -jnp.inf)
                    s_buf[:, j * HD : (j + 1) * HD] = s_half
                    best = jnp.maximum(best, s_half)
            best = jnp.broadcast_to(jnp.max(best, axis=1, keepdims=True), (tile, HD))
            total = jnp.zeros((tile, HD), F32)
            weighted = jnp.zeros((tile, HD), F32)
            for c in range(chips):
                keys = kk[c * tile : (c + 1) * tile, :]
                slopes = lax.dot_general(both, keys, contract_last, preferred_element_type=F32)
                for half in range(2):
                    j = 2 * c + half
                    there = slice(j * HD, (j + 1) * HD)
                    w = jnp.exp2((s_buf[:, there] - best) * step)
                    tilted = w * slopes[:, half * HD : (half + 1) * HD]
                    total = total + w
                    weighted = weighted + tilted
                    wb_buf[:, there] = w.astype(BF16)
                    tb_buf[:, there] = tilted.astype(BF16)
            sums = jnp.dot(wb_buf[...], vv[...], preferred_element_type=F32)
            slope_part = jnp.dot(tb_buf[...], vv[:, 0:HD], preferred_element_type=F32)
            total = jnp.sum(total, axis=1, keepdims=True)
            weighted = jnp.sum(weighted, axis=1, keepdims=True) * math.sqrt(2.0)
            primal, spread = sums[:, 0:HD], sums[:, HD : 2 * HD]
            result = (slope_part * math.sqrt(2.0) + spread) / total - (weighted / total) * (
                primal / total
            )
            out_stage[at] = result.astype(BF16)
            for c in range(2):
                block = at * 2 + c
                src = out_stage.at[at, pl.ds(c * ROWS, ROWS), :]
                dst = attn.at[:, pl.ds(pl.multiple_of(my_head * HD, HD), HD)]

                @pl.when(block != me)
                def _():
                    remote((src, dst, send_out.at[block], recv_out), block).start()

                @pl.when(block == me)
                def _():
                    pltpu.make_async_copy(src, dst, recv_out).start()

    w_copy.wait()
    pltpu.make_async_copy(attn, attn, recv_out).wait()

    width = w_buf.shape[1]
    wide = width // 8
    for n in range(8):
        cols = slice(n * wide, (n + 1) * wide)
        projected = jnp.dot(attn[...], w_buf[:, cols], preferred_element_type=F32)
        branch_ref[0, :, cols] = (ls_ref[:, cols] * projected).astype(BF16)
        weighed = cot_ref[0, :, cols].astype(F32) * projected
        g_part[n : n + 1, :] = jnp.sum(weighed, axis=0, keepdims=True)

    def exchange(axis, index, size, src, dst, ssem, rsem):
        def copy_to(i):
            return pltpu.make_async_remote_copy(
                src_ref=src,
                dst_ref=dst.at[index],
                send_sem=ssem.at[i],
                recv_sem=rsem,
                device_id={axis: (index + i) % size},
                device_id_type=MESH,
            )

        @pl.loop(1, size)
        def _(i):
            copy_to(i).start()

        pltpu.make_async_copy(src, dst.at[index], rsem).start()
        pltpu.make_async_copy(dst, dst, rsem).wait()
        return copy_to

    copy_c = exchange("ctx", me, n_ctx, g_part, g_ctx, send_gc, recv_gc)
    acc = g_ctx[0]
    for i in range(1, n_ctx):
        acc = acc + g_ctx[i]
    g_sum[...] = acc
    copy_d = exchange("dp", me_dp, n_dp, g_sum, g_dp, send_gd, recv_gd)
    acc = g_dp[0]
    for i in range(1, n_dp):
        acc = acc + g_dp[i]
    acc = acc / math.sqrt(n_ctx * n_dp * ROWS)
    for n in range(8):
        grad_ref[:, n * wide : (n + 1) * wide] = acc[n : n + 1, :]

    @pl.loop(0, HEADS)
    def _(h):
        to = owner_of(h)

        @pl.when(to != me)
        def _():
            for piece in pieces(h):
                remote(piece, to).wait_send()

    @pl.when(is_owner)
    def _():
        @pl.loop(0, n_ctx)
        def _(block):
            @pl.when(block != me)
            def _():
                src = out_stage.at[block // 2, pl.ds((block % 2) * ROWS, ROWS), :]
                dst = attn.at[:, pl.ds(pl.multiple_of(my_head * HD, HD), HD)]
                remote((src, dst, send_out.at[block], recv_out), block).wait_send()

    @pl.loop(1, n_ctx)
    def _(i):
        copy_c(i).wait_send()

    @pl.loop(1, n_dp)
    def _(i):
        copy_d(i).wait_send()


def turn_tables(blocks):
    frequency = 10000.0 ** (-np.arange(HD // 2, dtype=np.float64) / (HD // 2))
    frequency = np.concatenate([frequency, frequency])
    inside = np.arange(ROWS, dtype=np.float64)[:, None] * frequency
    start = ROWS * np.arange(blocks, dtype=np.float64)[:, None] * frequency
    return (
        np.stack([np.cos(inside), np.sin(inside)]).astype(np.float32),
        np.stack([np.cos(start), np.sin(start)]).astype(np.float32),
    )


def solution(mesh):
    n_ctx, n_dp = mesh.shape["ctx"], mesh.shape["dp"]
    inside, start = turn_tables(n_ctx)

    def local(
        queries,
        keys,
        values,
        tangent_queries,
        tangent_keys,
        tangent_values,
        clip_ids,
        block_order,
        out_weight,
        layer_scale,
        cotangent,
    ):
        width = out_weight.shape[1]
        seq = n_ctx * ROWS
        tile = 2 * ROWS
        vmem = pl.BlockSpec(memory_space=pltpu.VMEM)
        anywhere = pl.BlockSpec(memory_space=pl.ANY)
        dma = pltpu.SemaphoreType.DMA
        branch, grad = pl.pallas_call(
            lambda *refs: kernel(n_ctx, n_dp, *refs),
            out_shape=(
                jax.ShapeDtypeStruct((1, ROWS, width), BF16),
                jax.ShapeDtypeStruct((1, width), F32),
            ),
            in_specs=[
                pl.BlockSpec(memory_space=pltpu.SMEM),
                vmem,
                vmem,
                anywhere,
                vmem,
                vmem,
                anywhere,
                vmem,
                vmem,
                vmem,
                anywhere,
                vmem,
                vmem,
            ],
            out_specs=(vmem, vmem),
            scratch_shapes=[
                pltpu.VMEM((HEADS, ROWS, 2 * HD), BF16),
                pltpu.VMEM((HEADS, ROWS, 2 * HD), BF16),
                pltpu.VMEM((8, HD), F32),
                pltpu.VMEM((seq, 2 * HD), BF16),
                pltpu.VMEM((seq, 2 * HD), BF16),
                pltpu.VMEM((seq, 2 * HD), BF16),
                pltpu.VMEM((n_ctx, 8, HD), F32),
                pltpu.VMEM((seq, HD), F32),
                pltpu.VMEM((tile, seq), F32),
                pltpu.VMEM((tile, seq), BF16),
                pltpu.VMEM((tile, seq), BF16),
                pltpu.VMEM((n_ctx // 2, tile, HD), BF16),
                pltpu.VMEM((ROWS, HEADS * HD), BF16),
                pltpu.VMEM((HEADS * HD, width), BF16),
                pltpu.VMEM((8, width // 8), F32),
                pltpu.VMEM((n_ctx, 8, width // 8), F32),
                pltpu.VMEM((8, width // 8), F32),
                pltpu.VMEM((n_dp, 8, width // 8), F32),
                dma,
                dma((HEADS,)),
                dma((HEADS,)),
                dma((HEADS,)),
                dma((HEADS,)),
                dma((HEADS,)),
                dma,
                dma,
                dma((n_ctx,)),
                dma,
                dma((n_ctx,)),
                dma,
                dma((n_ctx,)),
                dma,
                dma((n_dp,)),
                dma,
            ],
            compiler_params=pltpu.CompilerParams(
                collective_id=0,
                has_side_effects=True,
                vmem_limit_bytes=48 * 1024 * 1024,
            ),
        )(
            block_order,
            queries,
            keys,
            values,
            tangent_queries,
            tangent_keys,
            tangent_values,
            clip_ids,
            jnp.asarray(inside),
            jnp.asarray(start),
            out_weight,
            layer_scale.reshape(1, width),
            cotangent,
        )
        return branch, grad.reshape(width)

    tokens = P("dp", "ctx", None)
    in_specs = (tokens,) * 6 + (P("dp", "ctx"), P(), P(), P(), tokens)
    return jax.shard_map(
        local, mesh=mesh, in_specs=in_specs, out_specs=(tokens, P()), check_vma=False
    )
```

time: 630 us -> 93.6 us (0.15)
  waiting for transfers between devices: 240 us -> 0 us
  matrix products: 150 us -> 0 us
  blocking collectives: 102 us -> 0 us
  Pallas kernels: 0 us -> 80.2 us
  local copies, waits for them, and re-layouts: 74 us -> 12.2 us
  other arithmetic: 41 us -> 0 us
  between operations: 14.6 us -> 0.66 us
    all_gather x4 -> x0, waiting for transfers between devices: 240 us -> none  [the longest x1 67.1 us: local(): value_part = lax.all_gather(value_heads, 'ctx', axis=1, tiled=True)]
    dot_general x97 -> x0, matrix products: 150 us -> none  [the longest x16 25.1 us: attend(): jnp.einsum('hqk,hkd->hqd', weights_b, value_blk, preferred_element_type=j...]
    pallas_call x0 -> x1, Pallas kernels: none -> 80.2 us  [local(): pl.pallas_call(lambda *refs: kernel(n_ctx, n_dp, *refs), out_shape=(jax.S...]
    psum x1 -> x0, blocking collectives: 75.7 us -> none  [local(): summed = lax.psum(partial_grad, ('ctx', 'dp'))]
    all_gather x3 -> x0, local copies, waits for them, and re-layouts: 26 us -> none  [the longest x1 8.67 us: local(): tvalue_part = lax.all_gather(tvalue_heads, 'ctx', axis=1, tiled=True)]
    all_gather x1 -> x0, blocking collectives: 25.8 us -> none  [local(): all_ids = lax.all_gather(clip_ids, 'ctx', axis=1, tiled=True)[0]]
    add x32 -> x0, other arithmetic: 20.5 us -> none  [the longest x16 20.4 us: attend(): weighted = weighted * factor + jnp.sum(tilted, axis=-1)]
    dynamic_slice x17 -> x0, local copies, waits for them, and re-layouts: 12.1 us -> none  [the longest x16 10.9 us: local(): carry, unused = lax.scan(attend, carry, stacked)]
  transfers between devices with their start and end apart: 4 -> 0, of which waited for: 4 -> 0; matrix products, arithmetic and copies ran while one was open for 6% -> 0% of each run, Pallas kernels for 0% -> 0%
where the time goes in v1:
time: 93.6 us; the launch traced here: 93.1 us
  Pallas kernels  80.2 us (86%)
  local copies, waits for them, and re-layouts  12.2 us (13%)
    pallas_call x1, Pallas kernels, local(): pl.pallas_call(lambda *refs: kernel(n_ctx, n_dp, *refs), out_shape=(jax.S...  80.2 us
    unnamed x26, local copies, waits for them, and re-layouts  12.2 us

profile of v1, /device:TPU:1, one launch (start us, length us, event | category | flops | bytes accessed | tf_op | source)
XLA Modules:
  0.0 93.1 jit_solution(2732872188846704989)
XLA Ops:
  0.6 0.0 copy-start
  0.6 1.1 %copy-done = bf16[1,128,3072]{2,1,0:T(8,128)(2,1)S(1)} copy-done((bf16[1,128,3072]{2,1,0:T(8,128)(2,1)S(1)}, bf16[1,128,3072]{2,1,0:T(8,128)(2,1)}, u32[]{:S(2)}) %copy-start) | copy-done | bytes 786456
  1.8 0.0 copy-start.1
  1.8 1.0 %copy-done.1 = bf16[1,128,1536]{2,1,0:T(8,128)(2,1)S(1)} copy-done((bf16[1,128,1536]{2,1,0:T(8,128)(2,1)S(1)}, bf16[1,128,1536]{2,1,0:T(8,128)(2,1)}, u32[]{:S(2)}) %copy-start.1) | copy-done | bytes 393240
  2.8 0.0 copy-start.2
  2.8 1.0 %copy-done.2 = bf16[1,128,1536]{2,1,0:T(8,128)(2,1)S(1)} copy-done((bf16[1,128,1536]{2,1,0:T(8,128)(2,1)S(1)}, bf16[1,128,1536]{2,1,0:T(8,128)(2,1)}, u32[]{:S(2)}) %copy-start.2) | copy-done | bytes 393240
  3.8 0.0 copy-start.3
  3.8 1.0 %copy-done.3 = bf16[1,128,1536]{2,1,0:T(8,128)(2,1)S(1)} copy-done((bf16[1,128,1536]{2,1,0:T(8,128)(2,1)S(1)}, bf16[1,128,1536]{2,1,0:T(8,128)(2,1)}, u32[]{:S(2)}) %copy-start.3) | copy-done | bytes 393240
  4.8 0.0 copy-start.4
  4.8 1.0 %copy-done.4 = bf16[1,128,1536]{2,1,0:T(8,128)(2,1)S(1)} copy-done((bf16[1,128,1536]{2,1,0:T(8,128)(2,1)S(1)}, bf16[1,128,1536]{2,1,0:T(8,128)(2,1)}, u32[]{:S(2)}) %copy-start.4) | copy-done | bytes 393240
  5.8 0.0 copy-start.5
  5.8 1.0 %copy-done.5 = bf16[1,128,1536]{2,1,0:T(8,128)(2,1)S(1)} copy-done((bf16[1,128,1536]{2,1,0:T(8,128)(2,1)S(1)}, bf16[1,128,1536]{2,1,0:T(8,128)(2,1)}, u32[]{:S(2)}) %copy-start.5) | copy-done | bytes 393240
  6.8 0.0 copy-start.6
  6.8 1.0 %copy-done.6 = bf16[1,128,1536]{2,1,0:T(8,128)(2,1)S(1)} copy-done((bf16[1,128,1536]{2,1,0:T(8,128)(2,1)S(1)}, bf16[1,128,1536]{2,1,0:T(8,128)(2,1)}, u32[]{:S(2)}) %copy-start.6) | copy-done | bytes 393240
  7.7 0.0 copy-start.7
  7.7 0.9 copy-done.7
  8.7 0.0 copy-start.8
  8.7 0.7 copy-done.8
  9.4 0.0 copy-start.9
  9.4 0.7 copy-done.9
  10.1 0.0 copy-start.10
  10.1 0.7 copy-done.10
  10.7 0.0 copy-start.11
  10.7 0.7 copy-done.11
  11.4 80.2 %shard_map.140 = (bf16[1,128,3072]{2,1,0:T(8,128)(2,1)S(1)}, f32[1,3072]{1,0:T(1,128)S(1)}) custom-call(s32[16]{0:T(128)S(1)} %copy-done.10, bf16[1,128,1536]{2,1,0:T(8,128)(2,1)S(1)} %copy-done.1, bf16[1,128,1536]{2,1,0:T(8,128)(2,1)S(1)} %copy-done.2, bf16[1,128,1536]{2,1,0:T(8,128)(2,1)S(1)} %copy-done.3, bf16[1,128,1536]{2,1,0:T(8,128)(2,1)S(1)} %copy-done.4, ...), custom_call_target="tpu_custom_call" | custom-call | tf_op jit(solution)/shard_map/pallas_call | solution.py:351
  91.6 0.9 copy.17
  92.5 0.6 copy.18
Async XLA Ops:
  0.6 1.1 %copy-start = (bf16[1,128,3072]{2,1,0:T(8,128)(2,1)S(1)}, bf16[1,128,3072]{2,1,0:T(8,128)(2,1)}, u32[]{:S(2)}) copy-start(bf16[1,128,3072]{2,1,0:T(8,128)(2,1)} %refs_12_.1) | copy-start | bytes 2359300
  1.8 1.0 %copy-start.1 = (bf16[1,128,1536]{2,1,0:T(8,128)(2,1)S(1)}, bf16[1,128,1536]{2,1,0:T(8,128)(2,1)}, u32[]{:S(2)}) copy-start(bf16[1,128,1536]{2,1,0:T(8,128)(2,1)} %refs_1_.1) | copy-start | bytes 1179652
  2.8 1.0 %copy-start.2 = (bf16[1,128,1536]{2,1,0:T(8,128)(2,1)S(1)}, bf16[1,128,1536]{2,1,0:T(8,128)(2,1)}, u32[]{:S(2)}) copy-start(bf16[1,128,1536]{2,1,0:T(8,128)(2,1)} %refs_2_.1) | copy-start | bytes 1179652
  3.8 1.0 %copy-start.3 = (bf16[1,128,1536]{2,1,0:T(8,128)(2,1)S(1)}, bf16[1,128,1536]{2,1,0:T(8,128)(2,1)}, u32[]{:S(2)}) copy-start(bf16[1,128,1536]{2,1,0:T(8,128)(2,1)} %refs_3_.1) | copy-start | bytes 1179652
  4.8 1.0 %copy-start.4 = (bf16[1,128,1536]{2,1,0:T(8,128)(2,1)S(1)}, bf16[1,128,1536]{2,1,0:T(8,128)(2,1)}, u32[]{:S(2)}) copy-start(bf16[1,128,1536]{2,1,0:T(8,128)(2,1)} %refs_4_.1) | copy-start | bytes 1179652
  5.8 1.0 %copy-start.5 = (bf16[1,128,1536]{2,1,0:T(8,128)(2,1)S(1)}, bf16[1,128,1536]{2,1,0:T(8,128)(2,1)}, u32[]{:S(2)}) copy-start(bf16[1,128,1536]{2,1,0:T(8,128)(2,1)} %refs_5_.1) | copy-start | bytes 1179652
  6.8 1.0 %copy-start.6 = (bf16[1,128,1536]{2,1,0:T(8,128)(2,1)S(1)}, bf16[1,128,1536]{2,1,0:T(8,128)(2,1)}, u32[]{:S(2)}) copy-start(bf16[1,128,1536]{2,1,0:T(8,128)(2,1)} %refs_6_.1) | copy-start | bytes 1179652
  7.7 0.9 copy-start.7
  8.7 0.7 copy-start.8
  9.4 0.7 copy-start.9
  10.1 0.7 copy-start.10
  10.7 0.7 copy-start.11

commit v2 on v1

--- a/solution.py
+++ b/solution.py
@@ -24,21 +24,29 @@
 def kernel(
     n_ctx,
     n_dp,
+    order_hbm,
+    q_hbm,
+    k_hbm,
+    v_ref,
+    tq_hbm,
+    tk_hbm,
+    tv_ref,
+    ids_hbm,
+    turn_hbm,
+    w_hbm,
+    ls_hbm,
+    cot_hbm,
+    branch_ref,
+    grad_ref,
     order_ref,
     q_ref,
     k_ref,
-    v_ref,
     tq_ref,
     tk_ref,
-    tv_ref,
     ids_ref,
     turn_ref,
-    block_turn_ref,
-    w_ref,
     ls_ref,
     cot_ref,
-    branch_ref,
-    grad_ref,
     kk_stage,
     qq_stage,
     id_stage,
@@ -57,7 +65,7 @@
     g_ctx,
     g_sum,
     g_dp,
-    w_sem,
+    load_sem,
     send_k,
     send_v,
     send_tv,
@@ -82,9 +90,6 @@
     is_owner = core * ((row + col) % 2) == 0
     chips = n_ctx // 2
 
-    w_copy = pltpu.make_async_copy(w_ref, w_buf, w_sem)
-    w_copy.start()
-
     barrier = pltpu.get_barrier_semaphore()
 
     @pl.loop(1, n_ctx)
@@ -99,10 +104,32 @@
             barrier, inc=1, device_id={"dp": (me_dp + i) % n_dp}, device_id_type=MESH
         )
 
+    loads = [
+        pltpu.make_async_copy(src, dst, load_sem.at[i])
+        for i, (src, dst) in enumerate(
+            [
+                (order_hbm, order_ref),
+                (turn_hbm, turn_ref),
+                (k_hbm, k_ref),
+                (tk_hbm, tk_ref),
+                (q_hbm, q_ref),
+                (tq_hbm, tq_ref),
+                (ids_hbm, ids_ref),
+                (ls_hbm, ls_ref),
+                (cot_hbm, cot_ref),
+                (w_hbm, w_buf),
+            ]
+        )
+    ]
+    for load in loads:
+        load.start()
+
+    for load in loads[:4]:
+        load.wait()
     place = order_ref[me]
-    cos_b = block_turn_ref[0, pl.ds(place, 1), :]
-    sin_b = block_turn_ref[1, pl.ds(place, 1), :]
-    cos_t, sin_t = turn_ref[0], turn_ref[1]
+    cos_b = turn_ref[0, pl.ds(ROWS + place, 1), :]
+    sin_b = turn_ref[1, pl.ds(ROWS + place, 1), :]
+    cos_t, sin_t = turn_ref[0, 0:ROWS, :], turn_ref[1, 0:ROWS, :]
     lane = lax.broadcasted_iota(jnp.int32, (ROWS, HD), 1)
     cosine = cos_b * cos_t - sin_b * sin_t
     sine = sin_b * cos_t + cos_b * sin_t
@@ -116,6 +143,8 @@
         cols = slice(h * HD, (h + 1) * HD)
         kk_stage[h, :, 0:HD] = turned(k_ref[0, :, cols], cosine, sine)
         kk_stage[h, :, HD : 2 * HD] = turned(tk_ref[0, :, cols], cosine, sine)
+    for load in loads[4:7]:
+        load.wait()
     cosine, sine = cosine * 0.0625, sine * 0.0625
     for h in range(HEADS):
         cols = slice(h * HD, (h + 1) * HD)
@@ -186,7 +215,7 @@
 
         @pl.loop(0, chips)
         def _(t):
-            at = (chip + t) % chips
+            at = (chip + chips - t) % chips
             rows = pl.ds(pl.multiple_of(at * tile, tile), tile)
             for c in range(2):
                 block = at * 2 + c
@@ -242,7 +271,8 @@
                 def _():
                     pltpu.make_async_copy(src, dst, recv_out).start()
 
-    w_copy.wait()
+    for load in loads[7:]:
+        load.wait()
     pltpu.make_async_copy(attn, attn, recv_out).wait()
 
     width = w_buf.shape[1]
@@ -284,7 +314,9 @@
         acc = acc + g_dp[i]
     acc = acc / math.sqrt(n_ctx * n_dp * ROWS)
     for n in range(8):
-        grad_ref[:, n * wide : (n + 1) * wide] = acc[n : n + 1, :]
+        for c in range(wide // HD):
+            at = n * (wide // HD) + c
+            grad_ref[at : at + 1, :] = acc[n : n + 1, c * HD : (c + 1) * HD]
 
     @pl.loop(0, HEADS)
     def _(h):
@@ -319,15 +351,13 @@
     frequency = np.concatenate([frequency, frequency])
     inside = np.arange(ROWS, dtype=np.float64)[:, None] * frequency
     start = ROWS * np.arange(blocks, dtype=np.float64)[:, None] * frequency
-    return (
-        np.stack([np.cos(inside), np.sin(inside)]).astype(np.float32),
-        np.stack([np.cos(start), np.sin(start)]).astype(np.float32),
-    )
+    angles = np.concatenate([inside, start])
+    return np.stack([np.cos(angles), np.sin(angles)]).astype(np.float32)
 
 
 def solution(mesh):
     n_ctx, n_dp = mesh.shape["ctx"], mesh.shape["dp"]
-    inside, start = turn_tables(n_ctx)
+    turns = turn_tables(n_ctx)
 
     def local(
         queries,
@@ -346,31 +376,25 @@
         seq = n_ctx * ROWS
         tile = 2 * ROWS
         vmem = pl.BlockSpec(memory_space=pltpu.VMEM)
-        anywhere = pl.BlockSpec(memory_space=pl.ANY)
         dma = pltpu.SemaphoreType.DMA
         branch, grad = pl.pallas_call(
             lambda *refs: kernel(n_ctx, n_dp, *refs),
             out_shape=(
                 jax.ShapeDtypeStruct((1, ROWS, width), BF16),
-                jax.ShapeDtypeStruct((1, width), F32),
+                jax.ShapeDtypeStruct((width // HD, HD), F32),
             ),
-            in_specs=[
-                pl.BlockSpec(memory_space=pltpu.SMEM),
-                vmem,
-                vmem,
-                anywhere,
-                vmem,
-                vmem,
-                anywhere,
-                vmem,
-                vmem,
-                vmem,
-                anywhere,
-                vmem,
-                vmem,
-            ],
+            in_specs=[pl.BlockSpec(memory_space=pltpu.HBM)] * 12,
             out_specs=(vmem, vmem),
             scratch_shapes=[
+                pltpu.SMEM((n_ctx,), jnp.int32),
+                pltpu.VMEM((1, ROWS, HEADS * HD), BF16),
+                pltpu.VMEM((1, ROWS, HEADS * HD), BF16),
+                pltpu.VMEM((1, ROWS, HEADS * HD), BF16),
+                pltpu.VMEM((1, ROWS, HEADS * HD), BF16),
+                pltpu.VMEM((1, ROWS), jnp.int32),
+                pltpu.VMEM((2, ROWS + n_ctx, HD), F32),
+                pltpu.VMEM((1, width), F32),
+                pltpu.VMEM((1, ROWS, width), BF16),
                 pltpu.VMEM((HEADS, ROWS, 2 * HD), BF16),
                 pltpu.VMEM((HEADS, ROWS, 2 * HD), BF16),
                 pltpu.VMEM((8, HD), F32),
@@ -389,7 +413,7 @@
                 pltpu.VMEM((n_ctx, 8, width // 8), F32),
                 pltpu.VMEM((8, width // 8), F32),
                 pltpu.VMEM((n_dp, 8, width // 8), F32),
-                dma,
+                dma((10,)),
                 dma((HEADS,)),
                 dma((HEADS,)),
                 dma((HEADS,)),
@@ -412,19 +436,20 @@
                 vmem_limit_bytes=48 * 1024 * 1024,
             ),
         )(
-            block_order,
-            queries,
-            keys,
-            values,
-            tangent_queries,
-            tangent_keys,
-            tangent_values,
-            clip_ids,
-            jnp.asarray(inside),
-            jnp.asarray(start),
-            out_weight,
-            layer_scale.reshape(1, width),
-            cotangent,
+            *[pltpu.with_memory_space_constraint(x, pltpu.HBM) for x in (
+                block_order,
+                queries,
+                keys,
+                values,
+                tangent_queries,
+                tangent_keys,
+                tangent_values,
+                clip_ids,
+                jnp.asarray(turns),
+                out_weight,
+                layer_scale.reshape(1, width),
+                cotangent,
+            )]
         )
         return branch, grad.reshape(width)
 

time: 93.6 us -> 81.8 us (0.87)
  local copies, waits for them, and re-layouts: 12.2 us -> 1.48 us
  Pallas kernels: 80.2 us -> 78.5 us
    unnamed x26 -> x2, local copies, waits for them, and re-layouts: 12.2 us -> 1.48 us
    pallas_call x1, Pallas kernels: 80.2 us -> 78.5 us  [local(): pl.pallas_call(lambda *refs: kernel(n_ctx, n_dp, *refs), out_shape=(jax.S...]
where the time goes in v2:
time: 81.8 us; the launch traced here: 80.6 us
  Pallas kernels  78.5 us (96%)
  local copies, waits for them, and re-layouts  1.48 us (2%)
    pallas_call x1, Pallas kernels, local(): pl.pallas_call(lambda *refs: kernel(n_ctx, n_dp, *refs), out_shape=(jax.S...  78.5 us

profile of v2, /device:TPU:1, one launch (start us, length us, event | category | flops | bytes accessed | tf_op | source)
XLA Modules:
  0.0 80.6 jit_solution(4296556059020451778)
XLA Ops:
  0.6 78.5 %shard_map.131 = (bf16[1,128,3072]{2,1,0:T(8,128)(2,1)S(1)}, f32[24,128]{1,0:T(8,128)S(1)}) custom-call(s32[16]{0:T(128)} %refs_0_.1, bf16[1,128,1536]{2,1,0:T(8,128)(2,1)} %refs_1_.1, bf16[1,128,1536]{2,1,0:T(8,128)(2,1)} %refs_2_.1, bf16[1,128,1536]{2,1,0:T(8,128)(2,1)} %refs_3_.1, bf16[1,128,1536]{2,1,0:T(8,128)(2,1)} %refs_4_.1, ...), custom_call_target="tpu_custom_call" | custom-call | tf_op jit(solution)/shard_map/pallas_call | solution.py:380
  79.1 0.9 %copy.16 = bf16[1,128,3072]{2,1,0:T(8,128)(2,1)} copy(bf16[1,128,3072]{2,1,0:T(8,128)(2,1)S(1)} %get-tuple-element.8) | data formatting | bytes 1572864
  80.0 0.6 copy.17

commit v3 on v2

--- a/solution.py
+++ b/solution.py
@@ -215,7 +215,7 @@
 
         @pl.loop(0, chips)
         def _(t):
-            at = (chip + chips - t) % chips
+            at = (chip + 2 * chips - 1 - t) % chips
             rows = pl.ds(pl.multiple_of(at * tile, tile), tile)
             for c in range(2):
                 block = at * 2 + c
@@ -282,7 +282,7 @@
         projected = jnp.dot(attn[...], w_buf[:, cols], preferred_element_type=F32)
         branch_ref[0, :, cols] = (ls_ref[:, cols] * projected).astype(BF16)
         weighed = cot_ref[0, :, cols].astype(F32) * projected
-        g_part[n : n + 1, :] = jnp.sum(weighed, axis=0, keepdims=True)
+        g_part[n : n + 1, :] = jnp.sum(weighed, axis=0, keepdims=True).astype(BF16)
 
     def exchange(axis, index, size, src, dst, ssem, rsem):
         def copy_to(i):
@@ -304,14 +304,14 @@
         return copy_to
 
     copy_c = exchange("ctx", me, n_ctx, g_part, g_ctx, send_gc, recv_gc)
-    acc = g_ctx[0]
+    acc = g_ctx[0].astype(F32)
     for i in range(1, n_ctx):
-        acc = acc + g_ctx[i]
-    g_sum[...] = acc
+        acc = acc + g_ctx[i].astype(F32)
+    g_sum[...] = acc.astype(BF16)
     copy_d = exchange("dp", me_dp, n_dp, g_sum, g_dp, send_gd, recv_gd)
-    acc = g_dp[0]
+    acc = g_dp[0].astype(F32)
     for i in range(1, n_dp):
-        acc = acc + g_dp[i]
+        acc = acc + g_dp[i].astype(F32)
     acc = acc / math.sqrt(n_ctx * n_dp * ROWS)
     for n in range(8):
         for c in range(wide // HD):
@@ -409,10 +409,10 @@
                 pltpu.VMEM((n_ctx // 2, tile, HD), BF16),
                 pltpu.VMEM((ROWS, HEADS * HD), BF16),
                 pltpu.VMEM((HEADS * HD, width), BF16),
-                pltpu.VMEM((8, width // 8), F32),
-                pltpu.VMEM((n_ctx, 8, width // 8), F32),
-                pltpu.VMEM((8, width // 8), F32),
-                pltpu.VMEM((n_dp, 8, width // 8), F32),
+                pltpu.VMEM((8, width // 8), BF16),
+                pltpu.VMEM((n_ctx, 8, width // 8), BF16),
+                pltpu.VMEM((8, width // 8), BF16),
+                pltpu.VMEM((n_dp, 8, width // 8), BF16),
                 dma((10,)),
                 dma((HEADS,)),
                 dma((HEADS,)),

time: 81.8 us -> 77.9 us (0.952); the launches traced: 80.6 us -> 77.9 us
  Pallas kernels: 78.5 us -> 75.7 us
    pallas_call x1, Pallas kernels: 78.5 us -> 75.7 us  [local(): pl.pallas_call(lambda *refs: kernel(n_ctx, n_dp, *refs), out_shape=(jax.S...]
where the time goes in v3:
time: 77.9 us
  Pallas kernels  75.7 us (97%)
  local copies, waits for them, and re-layouts  1.48 us (2%)
    pallas_call x1, Pallas kernels, local(): pl.pallas_call(lambda *refs: kernel(n_ctx, n_dp, *refs), out_shape=(jax.S...  75.7 us

profile of v3, /device:TPU:1, one launch (start us, length us, event | category | flops | bytes accessed | tf_op | source)
XLA Modules:
  0.0 77.9 jit_solution(6069105804388407654)
XLA Ops:
  0.6 75.7 %shard_map.131 = (bf16[1,128,3072]{2,1,0:T(8,128)(2,1)S(1)}, f32[24,128]{1,0:T(8,128)S(1)}) custom-call(s32[16]{0:T(128)} %refs_0_.1, bf16[1,128,1536]{2,1,0:T(8,128)(2,1)} %refs_1_.1, bf16[1,128,1536]{2,1,0:T(8,128)(2,1)} %refs_2_.1, bf16[1,128,1536]{2,1,0:T(8,128)(2,1)} %refs_3_.1, bf16[1,128,1536]{2,1,0:T(8,128)(2,1)} %refs_4_.1, ...), custom_call_target="tpu_custom_call" | custom-call | tf_op jit(solution)/shard_map/pallas_call | solution.py:380
  76.4 0.9 %copy.16 = bf16[1,128,3072]{2,1,0:T(8,128)(2,1)} copy(bf16[1,128,3072]{2,1,0:T(8,128)(2,1)S(1)} %get-tuple-element.8) | data formatting | bytes 1572864
  77.3 0.6 copy.17

commit v4 on v3

--- a/solution.py
+++ b/solution.py
@@ -58,6 +58,7 @@
     s_buf,
     wb_buf,
     tb_buf,
+    v_ones,
     out_stage,
     attn,
     w_buf,
@@ -206,8 +207,10 @@
             ids = jnp.broadcast_to(id_rows[j, 0:1, :], (ROWS, HD))
             id_cols[pl.ds(pl.multiple_of(j * ROWS, ROWS), ROWS), :] = ids.T
 
+        v_ones[:, HD : 2 * HD] = jnp.ones((n_ctx * ROWS, HD), BF16)
         pltpu.make_async_copy(kk, kk, recv_k).wait()
         pltpu.make_async_copy(vv, vv, recv_v).wait()
+        v_ones[:, 0:HD] = vv[:, 0:HD]
 
         tile = 2 * ROWS
         step = math.log2(math.e) * math.sqrt(2.0)
@@ -236,7 +239,6 @@
                     best = jnp.maximum(best, s_half)
             best = jnp.broadcast_to(jnp.max(best, axis=1, keepdims=True), (tile, HD))
             total = jnp.zeros((tile, HD), F32)
-            weighted = jnp.zeros((tile, HD), F32)
             for c in range(chips):
                 keys = kk[c * tile : (c + 1) * tile, :]
                 slopes = lax.dot_general(both, keys, contract_last, preferred_element_type=F32)
@@ -246,13 +248,13 @@
                     w = jnp.exp2((s_buf[:, there] - best) * step)
                     tilted = w * slopes[:, half * HD : (half + 1) * HD]
                     total = total + w
-                    weighted = weighted + tilted
                     wb_buf[:, there] = w.astype(BF16)
                     tb_buf[:, there] = tilted.astype(BF16)
             sums = jnp.dot(wb_buf[...], vv[...], preferred_element_type=F32)
-            slope_part = jnp.dot(tb_buf[...], vv[:, 0:HD], preferred_element_type=F32)
+            tilted_sums = jnp.dot(tb_buf[...], v_ones[...], preferred_element_type=F32)
+            slope_part = tilted_sums[:, 0:HD]
             total = jnp.sum(total, axis=1, keepdims=True)
-            weighted = jnp.sum(weighted, axis=1, keepdims=True) * math.sqrt(2.0)
+            weighted = tilted_sums[:, HD : 2 * HD] * math.sqrt(2.0)
             primal, spread = sums[:, 0:HD], sums[:, HD : 2 * HD]
             result = (slope_part * math.sqrt(2.0) + spread) / total - (weighted / total) * (
                 primal / total
@@ -406,6 +408,7 @@
                 pltpu.VMEM((tile, seq), F32),
                 pltpu.VMEM((tile, seq), BF16),
                 pltpu.VMEM((tile, seq), BF16),
+                pltpu.VMEM((seq, 2 * HD), BF16),
                 pltpu.VMEM((n_ctx // 2, tile, HD), BF16),
                 pltpu.VMEM((ROWS, HEADS * HD), BF16),
                 pltpu.VMEM((HEADS * HD, width), BF16),

time: 77.9 us -> 77.4 us (level)
  no operation moved by 1% of the time
where the time goes in v4:
time: 77.4 us
  Pallas kernels  75.2 us (97%)
  local copies, waits for them, and re-layouts  1.48 us (2%)
    pallas_call x1, Pallas kernels, local(): pl.pallas_call(lambda *refs: kernel(n_ctx, n_dp, *refs), out_shape=(jax.S...  75.2 us

profile of v4, /device:TPU:1, one launch (start us, length us, event | category | flops | bytes accessed | tf_op | source)
XLA Modules:
  0.0 77.4 jit_solution(1510768641310274172)
XLA Ops:
  0.6 75.2 %shard_map.131 = (bf16[1,128,3072]{2,1,0:T(8,128)(2,1)S(1)}, f32[24,128]{1,0:T(8,128)S(1)}) custom-call(s32[16]{0:T(128)} %refs_0_.1, bf16[1,128,1536]{2,1,0:T(8,128)(2,1)} %refs_1_.1, bf16[1,128,1536]{2,1,0:T(8,128)(2,1)} %refs_2_.1, bf16[1,128,1536]{2,1,0:T(8,128)(2,1)} %refs_3_.1, bf16[1,128,1536]{2,1,0:T(8,128)(2,1)} %refs_4_.1, ...), custom_call_target="tpu_custom_call" | custom-call | tf_op jit(solution)/shard_map/pallas_call | solution.py:382
  75.9 0.9 %copy.16 = bf16[1,128,3072]{2,1,0:T(8,128)(2,1)} copy(bf16[1,128,3072]{2,1,0:T(8,128)(2,1)S(1)} %get-tuple-element.8) | data formatting | bytes 1572864
  76.8 0.6 copy.17

commit v5 on v4

--- a/solution.py
+++ b/solution.py
@@ -195,8 +195,7 @@
                     src, dst, _, rsem = pieces(h)[p]
                     pltpu.make_async_copy(src, dst, rsem).start()
 
-    start_sends((0, 1, 2, 3))
-    start_sends((4,))
+    start_sends((0, 1, 4, 2, 3))
 
     @pl.when(is_owner)
     def _():

time: 77.4 us -> 80.5 us (1.040)
  Pallas kernels: 75.2 us -> 78.3 us
    pallas_call x1, Pallas kernels: 75.2 us -> 78.3 us  [local(): pl.pallas_call(lambda *refs: kernel(n_ctx, n_dp, *refs), out_shape=(jax.S...]
where the time goes in v5:
time: 80.5 us; the launch traced here: 80.4 us
  Pallas kernels  78.3 us (97%)
  local copies, waits for them, and re-layouts  1.48 us (2%)
    pallas_call x1, Pallas kernels, local(): pl.pallas_call(lambda *refs: kernel(n_ctx, n_dp, *refs), out_shape=(jax.S...  78.3 us

profile of v5, /device:TPU:1, one launch (start us, length us, event | category | flops | bytes accessed | tf_op | source)
XLA Modules:
  0.0 80.4 jit_solution(2473798796341714750)
XLA Ops:
  0.6 78.3 %shard_map.131 = (bf16[1,128,3072]{2,1,0:T(8,128)(2,1)S(1)}, f32[24,128]{1,0:T(8,128)S(1)}) custom-call(s32[16]{0:T(128)} %refs_0_.1, bf16[1,128,1536]{2,1,0:T(8,128)(2,1)} %refs_1_.1, bf16[1,128,1536]{2,1,0:T(8,128)(2,1)} %refs_2_.1, bf16[1,128,1536]{2,1,0:T(8,128)(2,1)} %refs_3_.1, bf16[1,128,1536]{2,1,0:T(8,128)(2,1)} %refs_4_.1, ...), custom_call_target="tpu_custom_call" | custom-call | tf_op jit(solution)/shard_map/pallas_call | solution.py:381
  78.9 0.9 %copy.16 = bf16[1,128,3072]{2,1,0:T(8,128)(2,1)} copy(bf16[1,128,3072]{2,1,0:T(8,128)(2,1)S(1)} %get-tuple-element.8) | data formatting | bytes 1572864
  79.8 0.6 copy.17
